TPU v7x, 32 devices: a whole 2x2x4 slice. The times are simulated.
32 devices in a mesh: dp: 8 (over z, x), chan: 4 (over y, core).
Axes of the slice: x: 2, y: 2, z: 4, core: 2. Of those that a mesh axis runs over, the one named last changes fastest.
Arguments:
- activations: bfloat16 [640, 32768], P('chan', 'dp'), may hold values from -6 to 6
- out_grad: bfloat16 [640, 32768], P('chan', 'dp'), may hold values from -6 to 6
- kernel: bfloat16 [640, 5760], P('chan'), may hold values from -0.078125 to 0.078125
- error_in: float32 [8, 640, 5760], P('dp', 'chan'), may hold values from -6 to 6
- q_prev: float32 [640, 4], P('chan'), may hold values from -6 to 6
Outputs:
- in_grad: bfloat16 [640, 32768], P('chan', 'dp')
- q_factor: float32 [640, 4], P('chan')
- new_error: float32 [8, 640, 5760], P('dp', 'chan')
All inputs are finite; a program needn't handle non-finite values.
Results may differ from a plain program's by a relative error of at most 0.001.
Values may be sent and summed in bfloat16 or wider, within the bound.
A program may use at most 128 MiB of HBM per device.

v0:
```python
import functools

import jax
import jax.numpy as jnp
from jax import lax
from jax.experimental import pallas as pl
from jax.experimental.pallas import tpu as pltpu
from jax.sharding import PartitionSpec as P

TAPS = 9
LANES = 128
SUB = 8
X_PARTS = 4
G_PARTS = 8
GROUP = 8
HI = lax.Precision.HIGHEST
F32 = jnp.float32
BF16 = jnp.bfloat16


def kernel_body(
    dims,
    x_hbm, g_hbm, k_hbm, e_hbm, qt_ref,
    in_grad_ref, qf_ref, err_hbm,
    x_all, g_all, stack, n_ref, e_vm, k_vm, k_send, k_all, kt, v_buf,
    s_buf, s_in, share, share_in, s_full, b_ref, f_buf, wide_q,
    local_sem, xs_y, xr_y, xs_c, xr_c, xs_f, xr_f,
    gs_y, gr_y, gs_c, gr_c, gs_f, gr_f, ks, kr,
    ss, sr, cs, cr, as_, ar, fs, fr, bs, br,
):
    n_dp, n_chan, side, rank, pieces = dims
    ch, cells = x_hbm.shape
    channels = ch * n_chan
    dp = lax.axis_index("dp")
    me = lax.axis_index("chan")
    core = me + 1 - 2 * lax.rem(me, 2)
    far = lax.rem(me + 2, n_chan)
    diag = lax.rem(core + 2, n_chan)
    tiles = channels * TAPS // LANES
    tap_tiles = channels // LANES

    def dp_peer(i):
        return lax.rem(dp + i, n_dp)

    def ch_peer(i):
        return lax.rem(me + i, n_chan)

    barrier = pltpu.get_barrier_semaphore()
    for i in range(1, n_chan):
        pl.semaphore_signal(barrier, inc=1, device_id={"chan": ch_peer(i)}, device_id_type=pl.DeviceIdType.MESH)

    @pl.loop(1, n_dp)
    def _(i):
        pl.semaphore_signal(barrier, inc=1, device_id={"dp": dp_peer(i)}, device_id_type=pl.DeviceIdType.MESH)

    def remote(src, dst, send, recv, where):
        return pltpu.make_async_remote_copy(
            src_ref=src, dst_ref=dst, send_sem=send, recv_sem=recv,
            device_id=where, device_id_type=pl.DeviceIdType.MESH,
        )

    local = [
        pltpu.make_async_copy(g_hbm, g_all.at[me], local_sem.at[0]),
        pltpu.make_async_copy(k_hbm, k_vm, local_sem.at[1]),
        pltpu.make_async_copy(x_hbm, x_all.at[me], local_sem.at[2]),
    ]
    for t in range(TAPS):
        local.append(pltpu.make_async_copy(e_hbm.at[0, :, pl.ds(t * channels, channels)], e_vm.at[t], local_sem.at[3 + t]))
    for c in local:
        c.start()

    pl.semaphore_wait(barrier, n_chan - 1 + n_dp - 1)

    xw = cells // X_PARTS
    gw = cells // G_PARTS

    def part(k, w):
        return pl.ds(pl.multiple_of(k * w, LANES), w)

    def x_copy(kind, k):
        s = part(k, xw)
        if kind == "y":
            return remote(x_hbm.at[:, s], x_all.at[me, :, s], xs_y.at[k], xr_y.at[k], {"chan": far})
        if kind == "c":
            return remote(x_hbm.at[:, s], x_all.at[me, :, s], xs_c.at[k], xr_c.at[k], {"chan": core})
        return remote(x_all.at[far, :, s], x_all.at[far, :, s], xs_f.at[k], xr_f.at[k], {"chan": core})

    def g_copy(kind, k):
        s = part(k, gw)
        if kind == "y":
            return remote(g_hbm.at[:, s], g_all.at[me, :, s], gs_y.at[k], gr_y.at[k], {"chan": far})
        if kind == "c":
            return remote(g_hbm.at[:, s], g_all.at[me, :, s], gs_c.at[k], gr_c.at[k], {"chan": core})
        return remote(g_all.at[far, :, s], g_all.at[far, :, s], gs_f.at[k], gr_f.at[k], {"chan": core})

    x_copy("y", 0).start()
    for k in range(X_PARTS):
        x_copy("c", k).start()

    local[1].wait()
    for j in range(n_chan):
        for t in range(TAPS):
            k_send[j, :, t * ch:(t + 1) * ch] = k_vm[:, t * channels + j * ch:t * channels + (j + 1) * ch]
        k_send[j, :, TAPS * ch:] = jnp.zeros((ch, k_send.shape[2] - TAPS * ch), BF16)

    turn = lax.rem(dp, GROUP)
    first = dp - turn
    quarters = GROUP // 2
    k_width = k_send.shape[2] // quarters
    across = far + (diag - far) * (turn // quarters)
    k_lanes = part(lax.rem(turn, quarters), k_width)

    def k_core():
        return remote(k_send.at[core], k_all.at[me], ks.at[0], kr.at[0], {"chan": core})

    def k_across():
        return remote(k_send.at[across, :, k_lanes], k_all.at[me, :, k_lanes], ks.at[1], kr.at[1], {"chan": across})

    def k_share(i):
        block = k_all.at[across, :, k_lanes]
        return remote(block, block, bs.at[i - 1], br.at[i - 1], {"dp": first + lax.rem(turn + i, GROUP)})

    k_across().start()
    for k in range(1, X_PARTS):
        x_copy("y", k).start()
    k_core().start()
    local[0].wait()
    rows = 16

    @pl.loop(0, ch // rows)
    def _(i):
        at = pl.ds(pl.multiple_of(i * rows, rows), rows)
        src = g_all[me, at, :].astype(F32)
        cell = lax.broadcasted_iota(jnp.int32, (1, cells), 1)
        col = cell % side
        row = cell // side
        for b in range(3):
            if b == 0:
                h = pltpu.roll(jnp.where(col != 0, src, 0.0), cells - 1, 1)
            elif b == 2:
                h = pltpu.roll(jnp.where(col != side - 1, src, 0.0), 1, 1)
            else:
                h = src
            for a in range(3):
                if a == 0:
                    v = pltpu.roll(jnp.where(row != 0, h, 0.0), cells - side, 1)
                elif a == 2:
                    v = pltpu.roll(jnp.where(row != side - 1, h, 0.0), side, 1)
                else:
                    v = h
                stack[3 * a + b, at, :] = v.astype(BF16)

    k_across().wait_recv()
    for i in range(1, GROUP):
        k_share(i).start()
    for k in range(G_PARTS):
        g_copy("c", k).start()
    early = G_PARTS // 2
    for k in range(early):
        g_copy("y", k).start()

    k_all[me] = k_send[me]

    def spread(rows_t):
        pad_c = f_buf.shape[2] - ch
        square = jnp.concatenate([rows_t, jnp.zeros((rows_t.shape[0], pad_c), F32)], axis=1) if pad_c else rows_t
        square = jnp.concatenate([square, jnp.zeros((LANES - rows_t.shape[0], square.shape[1]), F32)], axis=0)
        turned = jnp.transpose(square)[:ch]
        for r in range(rank):
            wide_q[r] = jnp.broadcast_to(turned[:, r:r + 1], (ch, LANES))

    spread(qt_ref[...])
    for a in range(3):
        v_buf[a, :, :LANES] = jnp.zeros((ch, LANES), F32)
        v_buf[a, :, LANES + cells:] = jnp.zeros((ch, LANES), F32)

    local[2].wait()

    @pl.loop(0, X_PARTS)
    def _(k):
        x_copy("y", k).wait_recv()
        x_copy("f", k).start()
        x_copy("c", k).wait_recv()
        x_copy("f", k).wait_recv()
        s = part(k, xw)
        for a in range(3):
            lhs = stack[3 * a:3 * a + 3, :, s].reshape(3 * ch, xw)
            rhs = x_all[:, :, s].reshape(channels, xw)
            out = lax.dot_general(lhs, rhs, (((1,), (1,)), ((), ())), preferred_element_type=F32).reshape(3, ch, channels)

            @pl.when(k == 0)
            def _():
                n_ref[3 * a:3 * a + 3] = out

            @pl.when(k > 0)
            def _():
                n_ref[3 * a:3 * a + 3] += out

    s_buf[tiles // pieces:] = jnp.zeros((n_dp - tiles // pieces, pieces, SUB, LANES), F32)
    for t in range(TAPS):
        local[3 + t].wait()
    for t in range(TAPS):
        for l in range(tap_tiles):
            at = t * tap_tiles + l
            lanes = slice(l * LANES, (l + 1) * LANES)
            value = n_ref[t, :, lanes] * (1.0 / side) + e_vm[t, :, lanes]
            n_ref[t, :, lanes] = value
            sums = [
                jnp.sum(jnp.sum((value * wide_q[r]).reshape(ch // SUB, SUB, LANES), axis=0), axis=0, keepdims=True)
                for r in range(rank)
            ]
            s_buf[at // pieces, at % pieces] = jnp.concatenate(sums + [jnp.zeros((SUB - rank, LANES), F32)], axis=0)

    def s_copy(i):
        peer = dp_peer(i)
        return remote(s_buf.at[peer], s_in.at[dp], ss.at[i - 1], sr.at[i - 1], {"dp": peer})

    @pl.loop(1, n_dp)
    def _(i):
        s_copy(i).start()

    for k in range(early, early + 2):
        g_copy("y", k).start()

    k_core().wait_recv()
    for i in range(1, GROUP):
        k_share(i).wait_recv()
    for i in range(k_all.shape[2] // LANES):
        block = k_all[:, :, i * LANES:(i + 1) * LANES].reshape(channels, LANES)
        kt[i * LANES:(i + 1) * LANES, :] = jnp.transpose(block)

    def forward_g(k):
        g_copy("y", k).wait_recv()
        g_copy("f", k).start()

    def in_grad_part(k):
        g_copy("c", k).wait_recv()
        g_copy("f", k).wait_recv()
        s = part(k, gw)
        col = lax.broadcasted_iota(jnp.int32, (1, gw), 1) % side
        for a in range(3):
            y = lax.dot_general(
                kt[3 * a * ch:(3 * a + 3) * ch, :], g_all[:, :, s].reshape(channels, gw),
                (((1,), (0,)), ((), ())), preferred_element_type=F32,
            )
            left = pltpu.roll(jnp.where(col != 0, y[:ch], 0.0), gw - 1, 1)
            right = pltpu.roll(jnp.where(col != side - 1, y[2 * ch:], 0.0), 1, 1)
            v_buf[a, :, pl.ds(pl.multiple_of(LANES + k * gw, LANES), gw)] = left + y[ch:2 * ch] + right

    def finish_part(k):
        base = k * gw
        wide = gw + LANES
        up = pltpu.roll(v_buf[0, :, pl.ds(pl.multiple_of(base + LANES, LANES), wide)], wide - side, 1)[:, :gw]
        down = pltpu.roll(v_buf[2, :, pl.ds(pl.multiple_of(base, LANES), wide)], wide - (LANES - side), 1)[:, :gw]
        mid = v_buf[1, :, pl.ds(pl.multiple_of(base + LANES, LANES), gw)]
        in_grad_ref[:, part(k, gw)] = (up + mid + down).astype(BF16)

    def run_parts(first, last):
        @pl.loop(first, last)
        def _(k):
            forward_g(k)
            in_grad_part(k)

    run_parts(0, 1)

    @pl.loop(1, n_dp)
    def _(i):
        s_copy(i).wait_recv()

    s_in[dp] = s_buf[dp]
    share[...] = lax.fori_loop(0, n_dp, lambda i, v: v + s_in[i], jnp.zeros(share.shape, F32))

    def c_copy(i):
        return remote(share, share_in.at[me], cs.at[i - 1], cr.at[i - 1], {"chan": ch_peer(i)})

    for i in range(1, n_chan):
        c_copy(i).start()
    share_in[me] = share[...]
    run_parts(1, 2)
    for i in range(1, n_chan):
        c_copy(i).wait_recv()
    total = share_in[0]
    for i in range(1, n_chan):
        total = total + share_in[i]
    s_full[dp] = total * (1.0 / n_dp)

    def a_copy(i):
        return remote(s_full.at[dp], s_full.at[dp], as_.at[i - 1], ar.at[i - 1], {"dp": dp_peer(i)})

    @pl.loop(1, n_dp)
    def _(i):
        a_copy(i).start()

    for k in range(early + 2, G_PARTS):
        g_copy("y", k).start()
    run_parts(2, 3)

    @pl.loop(1, n_dp)
    def _(i):
        a_copy(i).wait_recv()

    cols = [s_full[:, :, r, :] for r in range(rank)]

    def inner(u, v):
        return jnp.sum(u * v).reshape(1, 1, 1)

    gram = {}
    for i in range(rank):
        for j in range(i + 1):
            gram[i, j] = inner(cols[i], cols[j])
    low = {}
    for j in range(rank):
        d = gram[j, j]
        for m in range(j):
            d = d - low[j, m] * low[j, m]
        low[j, j] = jnp.sqrt(d)
        for i in range(j + 1, rank):
            d = gram[i, j]
            for m in range(j):
                d = d - low[i, m] * low[j, m]
            low[i, j] = d / low[j, j]
    base = []
    b_ref[...] = jnp.zeros(b_ref.shape, F32)
    for r in range(rank):
        v = cols[r]
        for m in range(r):
            v = v - low[r, m] * base[m]
        v = v / low[r, r]
        base.append(v)
        b_ref[:, :, r, :] = v

    lane = lax.broadcasted_iota(jnp.int32, (1, LANES), 1)
    half = ch // 4
    blocks = []
    for h in range(ch // half):
        acc = [jnp.zeros((half, LANES), F32) for _ in range(rank)]
        for t in range(TAPS):
            for l in range(tap_tiles):
                at = t * tap_tiles + l
                value = n_ref[t, h * half:(h + 1) * half, l * LANES:(l + 1) * LANES]
                for r in range(rank):
                    acc[r] = acc[r] + value * b_ref[at // pieces, at % pieces, r:r + 1, :]
        block = jnp.zeros((half, LANES), F32)
        for r in range(rank):
            block = jnp.where(lane == r, jnp.sum(acc[r], axis=1, keepdims=True), block)
        blocks.append(block)
    pad_c = f_buf.shape[2] - ch
    if pad_c:
        blocks.append(jnp.zeros((pad_c, LANES), F32))
    f_buf[dp] = jnp.transpose(jnp.concatenate(blocks, axis=0))[:SUB]

    def f_copy(i):
        return remote(f_buf.at[dp], f_buf.at[dp], fs.at[i - 1], fr.at[i - 1], {"dp": dp_peer(i)})

    @pl.loop(1, n_dp)
    def _(i):
        f_copy(i).start()

    run_parts(3, 4)

    @pl.loop(1, n_dp)
    def _(i):
        f_copy(i).wait_recv()

    fsum = lax.fori_loop(0, n_dp, lambda i, v: v + f_buf[i], jnp.zeros(f_buf.shape[1:], F32)) * (1.0 / n_dp)
    qf_ref[...] = fsum[:rank, :ch]
    spread(fsum[:rank, :ch])
    out_copies = []
    for t in range(TAPS):
        for l in range(tap_tiles):
            at = t * tap_tiles + l
            lanes = slice(l * LANES, (l + 1) * LANES)
            value = n_ref[t, :, lanes]
            for r in range(rank):
                value = value - wide_q[r] * b_ref[at // pieces, at % pieces, r:r + 1, :]
            n_ref[t, :, lanes] = value
        c = pltpu.make_async_copy(n_ref.at[t], err_hbm.at[0, :, pl.ds(t * channels, channels)], local_sem.at[3 + t])
        c.start()
        out_copies.append(c)

    run_parts(4, 5)

    @pl.loop(0, 4)
    def _(k):
        finish_part(k)

    @pl.loop(5, G_PARTS)
    def _(k):
        forward_g(k)
        in_grad_part(k)
        finish_part(k - 1)

    finish_part(G_PARTS - 1)

    for c in out_copies:
        c.wait()

    @pl.loop(0, X_PARTS)
    def _(k):
        x_copy("y", k).wait_send()
        x_copy("c", k).wait_send()
        x_copy("f", k).wait_send()

    @pl.loop(0, G_PARTS)
    def _(k):
        g_copy("y", k).wait_send()
        g_copy("c", k).wait_send()
        g_copy("f", k).wait_send()

    for i in range(1, n_chan):
        c_copy(i).wait_send()
    k_core().wait_send()
    k_across().wait_send()
    for i in range(1, GROUP):
        k_share(i).wait_send()

    @pl.loop(1, n_dp)
    def _(i):
        s_copy(i).wait_send()
        a_copy(i).wait_send()
        f_copy(i).wait_send()


def per_device(activations, out_grad, kernel, error_in, q_prev):
    n_dp = lax.axis_size("dp")
    n_chan = lax.axis_size("chan")
    ch, cells = activations.shape
    channels = kernel.shape[1] // TAPS
    rank = q_prev.shape[1]
    side = round(cells ** 0.5)
    tiles = channels * TAPS // LANES
    pieces = -(-tiles // n_dp)
    kw = -(-TAPS * ch // LANES) * LANES
    fw = -(-ch // LANES) * LANES
    qt = q_prev.T
    dma = pltpu.SemaphoreType.DMA
    anyspace = pl.BlockSpec(memory_space=pl.ANY)
    vmem = pl.BlockSpec(memory_space=pltpu.VMEM)
    in_grad, qf_t, new_error = pl.pallas_call(
        functools.partial(kernel_body, (n_dp, n_chan, side, rank, pieces)),
        out_shape=(
            jax.ShapeDtypeStruct((ch, cells), BF16),
            jax.ShapeDtypeStruct((rank, ch), F32),
            jax.ShapeDtypeStruct(error_in.shape, F32),
        ),
        in_specs=[anyspace, anyspace, anyspace, anyspace, vmem],
        out_specs=(vmem, vmem, anyspace),
        scratch_shapes=[
            pltpu.VMEM((n_chan, ch, cells), BF16),
            pltpu.VMEM((n_chan, ch, cells), BF16),
            pltpu.VMEM((TAPS, ch, cells), BF16),
            pltpu.VMEM((TAPS, ch, channels), F32),
            pltpu.VMEM((TAPS, ch, channels), F32),
            pltpu.VMEM(kernel.shape, BF16),
            pltpu.VMEM((n_chan, ch, kw), BF16),
            pltpu.VMEM((n_chan, ch, kw), BF16),
            pltpu.VMEM((kw, channels), BF16),
            pltpu.VMEM((3, ch, cells + 2 * LANES), F32),
            pltpu.VMEM((n_dp, pieces, SUB, LANES), F32),
            pltpu.VMEM((n_dp, pieces, SUB, LANES), F32),
            pltpu.VMEM((pieces, SUB, LANES), F32),
            pltpu.VMEM((n_chan, pieces, SUB, LANES), F32),
            pltpu.VMEM((n_dp, pieces, SUB, LANES), F32),
            pltpu.VMEM((n_dp, pieces, SUB, LANES), F32),
            pltpu.VMEM((n_dp, SUB, fw), F32),
            pltpu.VMEM((rank, ch, LANES), F32),
            dma((3 + TAPS,)),
        ]
        + [dma((X_PARTS,))] * 6
        + [dma((G_PARTS,))] * 6
        + [dma((n_chan - 1,))] * 2
        + [dma((n_dp - 1,))] * 2
        + [dma((n_chan - 1,))] * 2
        + [dma((n_dp - 1,))] * 4
        + [dma((GROUP - 1,))] * 2,
        compiler_params=pltpu.CompilerParams(
            collective_id=0, has_side_effects=True, vmem_limit_bytes=67000000
        ),
    )(activations, out_grad, kernel, error_in, qt)
    return in_grad, qf_t.T, new_error


def solution(mesh):
    in_specs = (
        P("chan", "dp"),
        P("chan", "dp"),
        P("chan", None),
        P("dp", "chan", None),
        P("chan", None),
    )
    out_specs = (P("chan", "dp"), P("chan", None), P("dp", "chan", None))
    return jax.shard_map(
        per_device, mesh=mesh, in_specs=in_specs, out_specs=out_specs, check_vma=False
    )
```

profile of v0, /device:TPU:0, one launch (start us, length us, event | category | flops | bytes accessed | tf_op | source)
XLA Modules:
  0.0 98.3 jit_solution(8321330286142484051)
XLA Ops:
  0.6 90.5 %shard_map.76 = (bf16[160,4096]{1,0:T(8,128)(2,1)}, f32[4,160]{1,0:T(4,128)}, f32[1,160,5760]{2,1,0:T(8,128)}) custom-call(bf16[160,4096]{1,0:T(8,128)(2,1)} %x_hbm.1, bf16[160,4096]{1,0:T(8,128)(2,1)} %g_hbm.1, bf16[160,5760]{1,0:T(8,128)(2,1)} %k_hbm.1, f32[1,160,5760]{2,1,0:T(8,128)} %e_hbm.1, f32[4,160]{1,0:T(4,128)} %bitcast.2), custom_call_target="tpu_custom_call" | custom-call | tf_op jit(solution)/shard_map/pallas_call | solution.py:439
  91.1 0.0 copy-start
  91.1 2.5 %copy.11 = bf16[160,4096]{1,0:T(8,128)(2,1)} copy(bf16[160,4096]{1,0:T(8,128)(2,1)} %get-tuple-element.12) | data formatting | bytes 2621440
  93.6 0.0 copy-done
  93.6 0.6 copy.12
  94.2 4.1 %copy.13 = f32[1,160,5760]{2,1,0:T(8,128)} copy(f32[1,160,5760]{2,1,0:T(8,128)} %get-tuple-element.14) | data formatting | bytes 7372800
Async XLA Ops:
  91.1 2.5 %copy-start = (f32[4,160]{1,0:T(4,128)S(1)}, f32[4,160]{1,0:T(4,128)}, u32[]{:S(2)}) copy-start(f32[4,160]{1,0:T(4,128)} %get-tuple-element.7) | copy-start | bytes 7684
where the time goes:
time: 98.5 us; the launch traced here: 98.3 us
  Pallas kernels  90.5 us (92%)
  local copies, waits for them, and re-layouts  7.21 us (7%)
    pallas_call x1, Pallas kernels, per_device(): pl.pallas_call(functools.partial(kernel_body, (n_dp, n_chan, side, rank,...  90.5 us
    unnamed x5, local copies, waits for them, and re-layouts  7.21 us

commit v1 on v0

--- a/solution.py
+++ b/solution.py
@@ -21,8 +21,8 @@
 def kernel_body(
     dims,
     x_hbm, g_hbm, k_hbm, e_hbm, qt_ref,
-    in_grad_ref, qf_ref, err_hbm,
-    x_all, g_all, stack, n_ref, e_vm, k_vm, k_send, k_all, kt, v_buf,
+    in_grad_ref, qf_ref, n_ref,
+    x_all, g_all, stack, e_vm, k_vm, k_send, k_all, kt, v_buf,
     s_buf, s_in, share, share_in, s_full, b_ref, f_buf, wide_q,
     local_sem, xs_y, xr_y, xs_c, xr_c, xs_f, xr_f,
     gs_y, gr_y, gs_c, gr_c, gs_f, gr_f, ks, kr,
@@ -365,7 +365,6 @@
     fsum = lax.fori_loop(0, n_dp, lambda i, v: v + f_buf[i], jnp.zeros(f_buf.shape[1:], F32)) * (1.0 / n_dp)
     qf_ref[...] = fsum[:rank, :ch]
     spread(fsum[:rank, :ch])
-    out_copies = []
     for t in range(TAPS):
         for l in range(tap_tiles):
             at = t * tap_tiles + l
@@ -374,9 +373,6 @@
             for r in range(rank):
                 value = value - wide_q[r] * b_ref[at // pieces, at % pieces, r:r + 1, :]
             n_ref[t, :, lanes] = value
-        c = pltpu.make_async_copy(n_ref.at[t], err_hbm.at[0, :, pl.ds(t * channels, channels)], local_sem.at[3 + t])
-        c.start()
-        out_copies.append(c)
 
     run_parts(4, 5)
 
@@ -391,9 +387,6 @@
         finish_part(k - 1)
 
     finish_part(G_PARTS - 1)
-
-    for c in out_copies:
-        c.wait()
 
     @pl.loop(0, X_PARTS)
     def _(k):
@@ -419,6 +412,20 @@
         s_copy(i).wait_send()
         a_copy(i).wait_send()
         f_copy(i).wait_send()
+
+
+def write_body(in_grad_vm, qf_vm, n_vm, in_grad_hbm, qf_hbm, err_hbm, sem):
+    channels = n_vm.shape[2]
+    copies = [
+        pltpu.make_async_copy(n_vm.at[t], err_hbm.at[0, :, pl.ds(t * channels, channels)], sem.at[t])
+        for t in range(TAPS)
+    ]
+    copies.append(pltpu.make_async_copy(in_grad_vm, in_grad_hbm, sem.at[TAPS]))
+    copies.append(pltpu.make_async_copy(qf_vm, qf_hbm, sem.at[TAPS + 1]))
+    for c in copies:
+        c.start()
+    for c in copies:
+        c.wait()
 
 
 def per_device(activations, out_grad, kernel, error_in, q_prev):
@@ -436,20 +443,19 @@
     dma = pltpu.SemaphoreType.DMA
     anyspace = pl.BlockSpec(memory_space=pl.ANY)
     vmem = pl.BlockSpec(memory_space=pltpu.VMEM)
-    in_grad, qf_t, new_error = pl.pallas_call(
+    held = pl.pallas_call(
         functools.partial(kernel_body, (n_dp, n_chan, side, rank, pieces)),
         out_shape=(
-            jax.ShapeDtypeStruct((ch, cells), BF16),
-            jax.ShapeDtypeStruct((rank, ch), F32),
-            jax.ShapeDtypeStruct(error_in.shape, F32),
+            pltpu.VMEM((ch, cells), BF16),
+            pltpu.VMEM((rank, ch), F32),
+            pltpu.VMEM((TAPS, ch, channels), F32),
         ),
         in_specs=[anyspace, anyspace, anyspace, anyspace, vmem],
-        out_specs=(vmem, vmem, anyspace),
+        out_specs=(vmem, vmem, vmem),
         scratch_shapes=[
             pltpu.VMEM((n_chan, ch, cells), BF16),
             pltpu.VMEM((n_chan, ch, cells), BF16),
             pltpu.VMEM((TAPS, ch, cells), BF16),
-            pltpu.VMEM((TAPS, ch, channels), F32),
             pltpu.VMEM((TAPS, ch, channels), F32),
             pltpu.VMEM(kernel.shape, BF16),
             pltpu.VMEM((n_chan, ch, kw), BF16),
@@ -474,9 +480,21 @@
         + [dma((n_dp - 1,))] * 4
         + [dma((GROUP - 1,))] * 2,
         compiler_params=pltpu.CompilerParams(
-            collective_id=0, has_side_effects=True, vmem_limit_bytes=67000000
+            collective_id=0, has_side_effects=True, vmem_limit_bytes=56000000
         ),
     )(activations, out_grad, kernel, error_in, qt)
+    in_grad, qf_t, new_error = pl.pallas_call(
+        write_body,
+        out_shape=(
+            jax.ShapeDtypeStruct((ch, cells), BF16),
+            jax.ShapeDtypeStruct((rank, ch), F32),
+            jax.ShapeDtypeStruct(error_in.shape, F32),
+        ),
+        in_specs=[vmem, vmem, vmem],
+        out_specs=(anyspace, anyspace, anyspace),
+        scratch_shapes=[dma((TAPS + 2,))],
+        compiler_params=pltpu.CompilerParams(vmem_limit_bytes=1000000),
+    )(*held)
     return in_grad, qf_t.T, new_error
 
 

time: 98.5 us -> 93.5 us (0.949)
  local copies, waits for them, and re-layouts: 7.21 us -> 0 us
  Pallas kernels: 90.5 us -> 92.5 us
    unnamed x5 -> x0, local copies, waits for them, and re-layouts: 7.21 us -> none
    pallas_call x0 -> x1, Pallas kernels: none -> 2.37 us  [per_device(): pl.pallas_call(write_body, out_shape=(jax.ShapeDtypeStruct((ch, cells), B...]
where the time goes in v1:
time: 93.5 us; the launch traced here: 93.3 us
  Pallas kernels  92.5 us (99%)
    pallas_call x1, Pallas kernels, per_device(): pl.pallas_call(functools.partial(kernel_body, (n_dp, n_chan, side, rank,...  90.1 us
    pallas_call x1, Pallas kernels, per_device(): pl.pallas_call(write_body, out_shape=(jax.ShapeDtypeStruct((ch, cells), B...  2.37 us

profile of v1, /device:TPU:0, one launch (start us, length us, event | category | flops | bytes accessed | tf_op | source)
XLA Modules:
  0.0 93.3 jit_solution(5923514165895794485)
XLA Ops:
  0.6 90.1 %shard_map.76 = (bf16[160,4096]{1,0:T(8,128)(2,1)S(1)}, f32[4,160]{1,0:T(4,128)S(1)}, f32[9,160,640]{2,1,0:T(8,128)S(1)}) custom-call(bf16[160,4096]{1,0:T(8,128)(2,1)} %x_hbm.1, bf16[160,4096]{1,0:T(8,128)(2,1)} %g_hbm.1, bf16[160,5760]{1,0:T(8,128)(2,1)} %k_hbm.1, f32[1,160,5760]{2,1,0:T(8,128)} %e_hbm.1, f32[4,160]{1,0:T(4,128)} %bitcast.2), custom_call_target="tpu_custom_call" | custom-call | tf_op jit(solution)/shard_map/pallas_call | solution.py:446
  90.8 2.4 %shard_map.77 = (bf16[160,4096]{1,0:T(8,128)(2,1)}, f32[4,160]{1,0:T(4,128)}, f32[1,160,5760]{2,1,0:T(8,128)}) custom-call(bf16[160,4096]{1,0:T(8,128)(2,1)S(1)} %get-tuple-element.9.in_grad_vm, f32[4,160]{1,0:T(4,128)S(1)} %get-tuple-element.10.qf_vm, f32[9,160,640]{2,1,0:T(8,128)S(1)} %get-tuple-element.11.n_vm), custom_call_target="tpu_custom_call" | custom-call | tf_op jit(solution)/shard_map/pallas_call | solution.py:486

commit v2 on v1

--- a/solution.py
+++ b/solution.py
@@ -10,8 +10,11 @@
 TAPS = 9
 LANES = 128
 SUB = 8
-X_PARTS = 4
+X_PARTS = 8
 G_PARTS = 8
+N_FIRST = 1
+N_SECOND = 2
+N_THIRD = 3
 GROUP = 8
 HI = lax.Precision.HIGHEST
 F32 = jnp.float32
@@ -24,8 +27,9 @@
     in_grad_ref, qf_ref, n_ref,
     x_all, g_all, stack, e_vm, k_vm, k_send, k_all, kt, v_buf,
     s_buf, s_in, share, share_in, s_full, b_ref, f_buf, wide_q,
+    p_own, p_core, p_half, p_in, p_taps, p_acc, p_wide,
     local_sem, xs_y, xr_y, xs_c, xr_c, xs_f, xr_f,
-    gs_y, gr_y, gs_c, gr_c, gs_f, gr_f, ks, kr,
+    gs_y, gr_y, gs_c, gr_c, gs_f, gr_f, ks, kr, ps, pr,
     ss, sr, cs, cr, as_, ar, fs, fr, bs, br,
 ):
     n_dp, n_chan, side, rank, pieces = dims
@@ -97,6 +101,54 @@
     for k in range(X_PARTS):
         x_copy("c", k).start()
 
+    def split3(v):
+        high = v.astype(BF16)
+        rest = v - high.astype(F32)
+        mid = rest.astype(BF16)
+        low = (rest - mid.astype(F32)).astype(BF16)
+        return high, mid, low
+
+    half = cells // 2
+    quarter = cells // 4
+    parity = lax.rem(me, 2)
+    pad_r = jnp.zeros((SUB - rank, ch), F32)
+    q_parts = [jnp.concatenate([v.astype(F32), pad_r], axis=0) for v in split3(qt_ref[...])]
+    q_rows = jnp.concatenate(q_parts + [jnp.zeros((SUB, ch), F32)], axis=0).astype(BF16)
+    local[0].wait()
+    p = lax.dot_general(q_rows, g_all[me], (((1,), (0,)), ((), ())), preferred_element_type=F32)
+    p = p[:SUB] + p[SUB:2 * SUB] + p[2 * SUB:3 * SUB]
+    p_own[:rank, :] = p[:rank, :half]
+    p_own[rank:, :] = p[:rank, half:]
+
+    def p_core_copy():
+        return remote(p_own, p_core, ps.at[0], pr.at[0], {"chan": core})
+
+    def p_far_copy():
+        return remote(p_half, p_in.at[parity], ps.at[1], pr.at[1], {"chan": far})
+
+    def p_diag_copy():
+        return remote(p_half, p_in.at[parity], ps.at[2], pr.at[2], {"chan": diag})
+
+    p_core_copy().start()
+
+    def spread(rows_t):
+        pad_c = f_buf.shape[2] - ch
+        square = jnp.concatenate([rows_t, jnp.zeros((rows_t.shape[0], pad_c), F32)], axis=1) if pad_c else rows_t
+        square = jnp.concatenate([square, jnp.zeros((LANES - rows_t.shape[0], square.shape[1]), F32)], axis=0)
+        turned = jnp.transpose(square)[:ch]
+        for r in range(rank):
+            wide_q[r] = jnp.broadcast_to(turned[:, r:r + 1], (ch, LANES))
+
+    spread(qt_ref[...])
+    p_core_copy().wait_recv()
+    both = p_own[...] + p_core[...]
+    p_half[...] = jnp.where(parity == 0, both[:, :quarter], both[:, quarter:])
+    p_far_copy().start()
+    p_diag_copy().start()
+    x_copy("y", 1).start()
+    for k in range(G_PARTS):
+        g_copy("c", k).start()
+
     local[1].wait()
     for j in range(n_chan):
         for t in range(TAPS):
@@ -106,9 +158,16 @@
     turn = lax.rem(dp, GROUP)
     first = dp - turn
     quarters = GROUP // 2
+    lines = GROUP // 2
+    line = turn // 2
+    pair = lax.rem(turn, 2)
     k_width = k_send.shape[2] // quarters
-    across = far + (diag - far) * (turn // quarters)
-    k_lanes = part(lax.rem(turn, quarters), k_width)
+
+    def k_piece(ln):
+        owner = far + (diag - far) * (ln // (lines // 2))
+        return owner, part(lax.rem(2 * ln + pair, quarters), k_width)
+
+    across, k_lanes = k_piece(line)
 
     def k_core():
         return remote(k_send.at[core], k_all.at[me], ks.at[0], kr.at[0], {"chan": core})
@@ -116,15 +175,20 @@
     def k_across():
         return remote(k_send.at[across, :, k_lanes], k_all.at[me, :, k_lanes], ks.at[1], kr.at[1], {"chan": across})
 
-    def k_share(i):
+    def k_line(i):
         block = k_all.at[across, :, k_lanes]
-        return remote(block, block, bs.at[i - 1], br.at[i - 1], {"dp": first + lax.rem(turn + i, GROUP)})
+        peer = first + 2 * lax.rem(line + i, lines) + pair
+        return remote(block, block, bs.at[i - 1], br.at[i - 1], {"dp": peer})
+
+    def k_pair(i):
+        owner, lanes = k_piece(lax.rem(line + lines - i, lines))
+        block = k_all.at[owner, :, lanes]
+        at = lines - 1 + i
+        return remote(block, block, bs.at[at], br.at[at], {"dp": first + 2 * line + 1 - pair})
 
     k_across().start()
-    for k in range(1, X_PARTS):
-        x_copy("y", k).start()
+    x_copy("y", 2).start()
     k_core().start()
-    local[0].wait()
     rows = 16
 
     @pl.loop(0, ch // rows)
@@ -150,51 +214,11 @@
                     v = h
                 stack[3 * a + b, at, :] = v.astype(BF16)
 
-    k_across().wait_recv()
-    for i in range(1, GROUP):
-        k_share(i).start()
-    for k in range(G_PARTS):
-        g_copy("c", k).start()
-    early = G_PARTS // 2
-    for k in range(early):
-        g_copy("y", k).start()
-
     k_all[me] = k_send[me]
 
-    def spread(rows_t):
-        pad_c = f_buf.shape[2] - ch
-        square = jnp.concatenate([rows_t, jnp.zeros((rows_t.shape[0], pad_c), F32)], axis=1) if pad_c else rows_t
-        square = jnp.concatenate([square, jnp.zeros((LANES - rows_t.shape[0], square.shape[1]), F32)], axis=0)
-        turned = jnp.transpose(square)[:ch]
-        for r in range(rank):
-            wide_q[r] = jnp.broadcast_to(turned[:, r:r + 1], (ch, LANES))
-
-    spread(qt_ref[...])
     for a in range(3):
         v_buf[a, :, :LANES] = jnp.zeros((ch, LANES), F32)
         v_buf[a, :, LANES + cells:] = jnp.zeros((ch, LANES), F32)
-
-    local[2].wait()
-
-    @pl.loop(0, X_PARTS)
-    def _(k):
-        x_copy("y", k).wait_recv()
-        x_copy("f", k).start()
-        x_copy("c", k).wait_recv()
-        x_copy("f", k).wait_recv()
-        s = part(k, xw)
-        for a in range(3):
-            lhs = stack[3 * a:3 * a + 3, :, s].reshape(3 * ch, xw)
-            rhs = x_all[:, :, s].reshape(channels, xw)
-            out = lax.dot_general(lhs, rhs, (((1,), (1,)), ((), ())), preferred_element_type=F32).reshape(3, ch, channels)
-
-            @pl.when(k == 0)
-            def _():
-                n_ref[3 * a:3 * a + 3] = out
-
-            @pl.when(k > 0)
-            def _():
-                n_ref[3 * a:3 * a + 3] += out
 
     s_buf[tiles // pieces:] = jnp.zeros((n_dp - tiles // pieces, pieces, SUB, LANES), F32)
     for t in range(TAPS):
@@ -202,15 +226,91 @@
     for t in range(TAPS):
         for l in range(tap_tiles):
             at = t * tap_tiles + l
-            lanes = slice(l * LANES, (l + 1) * LANES)
-            value = n_ref[t, :, lanes] * (1.0 / side) + e_vm[t, :, lanes]
-            n_ref[t, :, lanes] = value
+            value = e_vm[t, :, l * LANES:(l + 1) * LANES]
             sums = [
                 jnp.sum(jnp.sum((value * wide_q[r]).reshape(ch // SUB, SUB, LANES), axis=0), axis=0, keepdims=True)
                 for r in range(rank)
             ]
             s_buf[at // pieces, at % pieces] = jnp.concatenate(sums + [jnp.zeros((SUB - rank, LANES), F32)], axis=0)
 
+    p_far_copy().wait_recv()
+    p_diag_copy().wait_recv()
+    both = p_own[...] + p_core[...]
+    both = jnp.concatenate([both[:, :quarter] + p_in[0], both[:, quarter:] + p_in[1]], axis=1)
+    p = jnp.concatenate([both[:rank], both[rank:]], axis=1)
+    cell = lax.broadcasted_iota(jnp.int32, (1, cells), 1)
+    col = cell % side
+    row = cell // side
+    p_taps[TAPS * rank:] = jnp.zeros((p_taps.shape[0] - TAPS * rank, cells), F32)
+    for b in range(3):
+        if b == 0:
+            h = pltpu.roll(jnp.where(col != 0, p, 0.0), cells - 1, 1)
+        elif b == 2:
+            h = pltpu.roll(jnp.where(col != side - 1, p, 0.0), 1, 1)
+        else:
+            h = p
+        for a in range(3):
+            if a == 0:
+                v = pltpu.roll(jnp.where(row != 0, h, 0.0), cells - side, 1)
+            elif a == 2:
+                v = pltpu.roll(jnp.where(row != side - 1, h, 0.0), side, 1)
+            else:
+                v = h
+            t = 3 * a + b
+            p_taps[t * rank:(t + 1) * rank, :] = v
+
+    local[2].wait()
+    p_rows = p_taps.shape[0]
+    p_acc[...] = jnp.zeros(p_acc.shape, F32)
+
+    @pl.loop(0, X_PARTS)
+    def _(k):
+        s = part(k, xw)
+        lhs = jnp.concatenate(split3(p_taps[:, s]), axis=0)
+        p_acc[...] += lax.dot_general(lhs, x_all[me, :, s], (((1,), (1,)), ((), ())), preferred_element_type=F32)
+
+    first_sketch = (p_acc[:p_rows] + p_acc[p_rows:2 * p_rows] + p_acc[2 * p_rows:]) * (1.0 / side)
+    p_wide[...] = jnp.zeros(p_wide.shape, F32)
+    for j in range(n_chan):
+        @pl.when(me == j)
+        def _():
+            for t in range(TAPS):
+                p_wide[t, :rank, j * ch:(j + 1) * ch] = first_sketch[t * rank:(t + 1) * rank]
+
+    for t in range(TAPS):
+        for l in range(tap_tiles):
+            at = t * tap_tiles + l
+            s_buf[at // pieces, at % pieces] += p_wide[t, :, l * LANES:(l + 1) * LANES]
+
+    x_copy("y", 3).start()
+
+    def forward_x(k):
+        x_copy("y", k).wait_recv()
+        x_copy("f", k).start()
+
+    def run_n(first, last):
+        @pl.loop(first, last)
+        def _(k):
+            @pl.when(k + 1 < X_PARTS)
+            def _():
+                forward_x(k + 1)
+
+            x_copy("c", k).wait_recv()
+            x_copy("f", k).wait_recv()
+            s = part(k, xw)
+            for a in range(3):
+                lhs = stack[3 * a:3 * a + 3, :, s].reshape(3 * ch, xw)
+                rhs = x_all[:, :, s].reshape(channels, xw)
+                out = lax.dot_general(lhs, rhs, (((1,), (1,)), ((), ())), preferred_element_type=F32).reshape(3, ch, channels)
+
+                @pl.when(k == 0)
+                def _():
+                    n_ref[3 * a:3 * a + 3] = out
+
+                @pl.when(k > 0)
+                def _():
+                    n_ref[3 * a:3 * a + 3] += out
+
     def s_copy(i):
         peer = dp_peer(i)
         return remote(s_buf.at[peer], s_in.at[dp], ss.at[i - 1], sr.at[i - 1], {"dp": peer})
@@ -219,15 +319,13 @@
     def _(i):
         s_copy(i).start()
 
-    for k in range(early, early + 2):
-        g_copy("y", k).start()
-
-    k_core().wait_recv()
-    for i in range(1, GROUP):
-        k_share(i).wait_recv()
-    for i in range(k_all.shape[2] // LANES):
-        block = k_all[:, :, i * LANES:(i + 1) * LANES].reshape(channels, LANES)
-        kt[i * LANES:(i + 1) * LANES, :] = jnp.transpose(block)
+    forward_x(0)
+    run_n(0, N_FIRST)
+    x_copy("y", 4).start()
+    k_across().wait_recv()
+    for i in range(1, lines):
+        k_line(i).start()
+    k_pair(0).start()
 
     def forward_g(k):
         g_copy("y", k).wait_recv()
@@ -255,14 +353,6 @@
         mid = v_buf[1, :, pl.ds(pl.multiple_of(base + LANES, LANES), gw)]
         in_grad_ref[:, part(k, gw)] = (up + mid + down).astype(BF16)
 
-    def run_parts(first, last):
-        @pl.loop(first, last)
-        def _(k):
-            forward_g(k)
-            in_grad_part(k)
-
-    run_parts(0, 1)
-
     @pl.loop(1, n_dp)
     def _(i):
         s_copy(i).wait_recv()
@@ -276,7 +366,11 @@
     for i in range(1, n_chan):
         c_copy(i).start()
     share_in[me] = share[...]
-    run_parts(1, 2)
+    for k in range(5, X_PARTS):
+        x_copy("y", k).start()
+    for k in range(G_PARTS):
+        g_copy("y", k).start()
+    run_n(N_FIRST, N_SECOND)
     for i in range(1, n_chan):
         c_copy(i).wait_recv()
     total = share_in[0]
@@ -291,9 +385,7 @@
     def _(i):
         a_copy(i).start()
 
-    for k in range(early + 2, G_PARTS):
-        g_copy("y", k).start()
-    run_parts(2, 3)
+    run_n(N_SECOND, N_THIRD)
 
     @pl.loop(1, n_dp)
     def _(i):
@@ -329,6 +421,10 @@
         base.append(v)
         b_ref[:, :, r, :] = v
 
+    for i in range(1, lines):
+        k_line(i).wait_recv()
+        k_pair(i).start()
+    run_n(N_THIRD, X_PARTS)
     lane = lax.broadcasted_iota(jnp.int32, (1, LANES), 1)
     half = ch // 4
     blocks = []
@@ -337,7 +433,10 @@
         for t in range(TAPS):
             for l in range(tap_tiles):
                 at = t * tap_tiles + l
-                value = n_ref[t, h * half:(h + 1) * half, l * LANES:(l + 1) * LANES]
+                rows_h = slice(h * half, (h + 1) * half)
+                lanes = slice(l * LANES, (l + 1) * LANES)
+                value = n_ref[t, rows_h, lanes] * (1.0 / side) + e_vm[t, rows_h, lanes]
+                n_ref[t, rows_h, lanes] = value
                 for r in range(rank):
                     acc[r] = acc[r] + value * b_ref[at // pieces, at % pieces, r:r + 1, :]
         block = jnp.zeros((half, LANES), F32)
@@ -356,7 +455,12 @@
     def _(i):
         f_copy(i).start()
 
-    run_parts(3, 4)
+    k_core().wait_recv()
+    for i in range(lines):
+        k_pair(i).wait_recv()
+    for i in range(k_all.shape[2] // LANES):
+        block = k_all[:, :, i * LANES:(i + 1) * LANES].reshape(channels, LANES)
+        kt[i * LANES:(i + 1) * LANES, :] = jnp.transpose(block)
 
     @pl.loop(1, n_dp)
     def _(i):
@@ -374,17 +478,19 @@
                 value = value - wide_q[r] * b_ref[at // pieces, at % pieces, r:r + 1, :]
             n_ref[t, :, lanes] = value
 
-    run_parts(4, 5)
-
-    @pl.loop(0, 4)
+    forward_g(0)
+
+    @pl.loop(0, G_PARTS)
     def _(k):
-        finish_part(k)
-
-    @pl.loop(5, G_PARTS)
-    def _(k):
-        forward_g(k)
+        @pl.when(k + 1 < G_PARTS)
+        def _():
+            forward_g(k + 1)
+
         in_grad_part(k)
-        finish_part(k - 1)
+
+        @pl.when(k > 0)
+        def _():
+            finish_part(k - 1)
 
     finish_part(G_PARTS - 1)
 
@@ -404,8 +510,13 @@
         c_copy(i).wait_send()
     k_core().wait_send()
     k_across().wait_send()
-    for i in range(1, GROUP):
-        k_share(i).wait_send()
+    p_core_copy().wait_send()
+    p_far_copy().wait_send()
+    p_diag_copy().wait_send()
+    for i in range(1, lines):
+        k_line(i).wait_send()
+    for i in range(lines):
+        k_pair(i).wait_send()
 
     @pl.loop(1, n_dp)
     def _(i):
@@ -440,6 +551,7 @@
     kw = -(-TAPS * ch // LANES) * LANES
     fw = -(-ch // LANES) * LANES
     qt = q_prev.T
+    p_rows = -(-TAPS * rank // (2 * SUB)) * 2 * SUB
     dma = pltpu.SemaphoreType.DMA
     anyspace = pl.BlockSpec(memory_space=pl.ANY)
     vmem = pl.BlockSpec(memory_space=pltpu.VMEM)
@@ -470,11 +582,18 @@
             pltpu.VMEM((n_dp, pieces, SUB, LANES), F32),
             pltpu.VMEM((n_dp, SUB, fw), F32),
             pltpu.VMEM((rank, ch, LANES), F32),
+            pltpu.VMEM((2 * rank, cells // 2), F32),
+            pltpu.VMEM((2 * rank, cells // 2), F32),
+            pltpu.VMEM((2 * rank, cells // 4), F32),
+            pltpu.VMEM((2, 2 * rank, cells // 4), F32),
+            pltpu.VMEM((p_rows, cells), F32),
+            pltpu.VMEM((3 * p_rows, ch), F32),
+            pltpu.VMEM((TAPS, SUB, channels), F32),
             dma((3 + TAPS,)),
         ]
         + [dma((X_PARTS,))] * 6
         + [dma((G_PARTS,))] * 6
-        + [dma((n_chan - 1,))] * 2
+        + [dma((n_chan - 1,))] * 4
         + [dma((n_dp - 1,))] * 2
         + [dma((n_chan - 1,))] * 2
         + [dma((n_dp - 1,))] * 4

time: 93.5 us -> 80.6 us (0.86)
  Pallas kernels: 92.5 us -> 79.3 us
    pallas_call x1, Pallas kernels: 90.1 us -> 76.9 us  [per_device(): pl.pallas_call(functools.partial(kernel_body, (n_dp, n_chan, side, rank,...]
where the time goes in v2:
time: 80.6 us; the launch traced here: 80.1 us
  Pallas kernels  79.3 us (98%)
    pallas_call x1, Pallas kernels, per_device(): pl.pallas_call(functools.partial(kernel_body, (n_dp, n_chan, side, rank,...  76.9 us
    pallas_call x1, Pallas kernels, per_device(): pl.pallas_call(write_body, out_shape=(jax.ShapeDtypeStruct((ch, cells), B...  2.37 us

profile of v2, /device:TPU:0, one launch (start us, length us, event | category | flops | bytes accessed | tf_op | source)
XLA Modules:
  0.0 80.1 jit_solution(10882663306038684193)
XLA Ops:
  0.6 76.9 %shard_map.76 = (bf16[160,4096]{1,0:T(8,128)(2,1)S(1)}, f32[4,160]{1,0:T(4,128)S(1)}, f32[9,160,640]{2,1,0:T(8,128)S(1)}) custom-call(bf16[160,4096]{1,0:T(8,128)(2,1)} %x_hbm.1, bf16[160,4096]{1,0:T(8,128)(2,1)} %g_hbm.1, bf16[160,5760]{1,0:T(8,128)(2,1)} %k_hbm.1, f32[1,160,5760]{2,1,0:T(8,128)} %e_hbm.1, f32[4,160]{1,0:T(4,128)} %bitcast.2), custom_call_target="tpu_custom_call" | custom-call | tf_op jit(solution)/shard_map/pallas_call | solution.py:558
  77.5 2.4 %shard_map.77 = (bf16[160,4096]{1,0:T(8,128)(2,1)}, f32[4,160]{1,0:T(4,128)}, f32[1,160,5760]{2,1,0:T(8,128)}) custom-call(bf16[160,4096]{1,0:T(8,128)(2,1)S(1)} %get-tuple-element.9.in_grad_vm, f32[4,160]{1,0:T(4,128)S(1)} %get-tuple-element.10.qf_vm, f32[9,160,640]{2,1,0:T(8,128)S(1)} %get-tuple-element.11.n_vm), custom_call_target="tpu_custom_call" | custom-call | tf_op jit(solution)/shard_map/pallas_call | solution.py:605

commit v3 on v2

--- a/solution.py
+++ b/solution.py
@@ -21,16 +21,38 @@
 BF16 = jnp.bfloat16
 
 
+def tap_rows(side, kt, g_cols, v_buf, at):
+    ch = v_buf.shape[1]
+    gw = g_cols.shape[1]
+    col = lax.broadcasted_iota(jnp.int32, (1, gw), 1) % side
+    for a in range(3):
+        y = lax.dot_general(
+            kt[3 * a * ch:(3 * a + 3) * ch, :], g_cols,
+            (((1,), (0,)), ((), ())), preferred_element_type=F32,
+        )
+        left = pltpu.roll(jnp.where(col != 0, y[:ch], 0.0), gw - 1, 1)
+        right = pltpu.roll(jnp.where(col != side - 1, y[2 * ch:], 0.0), 1, 1)
+        v_buf[a, :, at] = left + y[ch:2 * ch] + right
+
+
+def finish_cells(side, v_buf, base, gw):
+    wide = gw + LANES
+    up = pltpu.roll(v_buf[0, :, pl.ds(pl.multiple_of(base + LANES, LANES), wide)], wide - side, 1)[:, :gw]
+    down = pltpu.roll(v_buf[2, :, pl.ds(pl.multiple_of(base, LANES), wide)], wide - (LANES - side), 1)[:, :gw]
+    mid = v_buf[1, :, pl.ds(pl.multiple_of(base + LANES, LANES), gw)]
+    return (up + mid + down).astype(BF16)
+
+
 def kernel_body(
     dims,
     x_hbm, g_hbm, k_hbm, e_hbm, qt_ref,
-    in_grad_ref, qf_ref, n_ref,
-    x_all, g_all, stack, e_vm, k_vm, k_send, k_all, kt, v_buf,
+    in_grad_ref, qf_ref, n_ref, g_all, kt, v_buf,
+    x_all, stack, e_vm, k_vm, k_send, k_all,
     s_buf, s_in, share, share_in, s_full, b_ref, f_buf, wide_q,
     p_own, p_core, p_half, p_in, p_taps, p_acc, p_wide,
     local_sem, xs_y, xr_y, xs_c, xr_c, xs_f, xr_f,
     gs_y, gr_y, gs_c, gr_c, gs_f, gr_f, ks, kr, ps, pr,
-    ss, sr, cs, cr, as_, ar, fs, fr, bs, br,
+    ss, sr, cs, cr, as_, ar, fs, fr, bs, br, here, go,
 ):
     n_dp, n_chan, side, rank, pieces = dims
     ch, cells = x_hbm.shape
@@ -42,6 +64,7 @@
     diag = lax.rem(core + 2, n_chan)
     tiles = channels * TAPS // LANES
     tap_tiles = channels // LANES
+    per = SUB // rank
 
     def dp_peer(i):
         return lax.rem(dp + i, n_dp)
@@ -50,12 +73,47 @@
         return lax.rem(me + i, n_chan)
 
     barrier = pltpu.get_barrier_semaphore()
+    root = (dp == 0) & (me == 0)
+
     for i in range(1, n_chan):
-        pl.semaphore_signal(barrier, inc=1, device_id={"chan": ch_peer(i)}, device_id_type=pl.DeviceIdType.MESH)
-
-    @pl.loop(1, n_dp)
-    def _(i):
-        pl.semaphore_signal(barrier, inc=1, device_id={"dp": dp_peer(i)}, device_id_type=pl.DeviceIdType.MESH)
+        @pl.when((dp != 0) | (ch_peer(i) != 0))
+        def _():
+            pl.semaphore_signal(barrier, inc=1, device_id={"chan": ch_peer(i)}, device_id_type=pl.DeviceIdType.MESH)
+
+    @pl.when(dp != 0)
+    def _():
+        pl.semaphore_signal(barrier, inc=1, device_id={"dp": 0, "chan": 0}, device_id_type=pl.DeviceIdType.MESH)
+
+    def enter_group():
+        @pl.when(jnp.logical_not(root))
+        def _():
+            pl.semaphore_wait(barrier, n_chan - 1)
+
+            @pl.when(dp == 0)
+            def _():
+                pl.semaphore_signal(here, inc=1, device_id={"chan": 0}, device_id_type=pl.DeviceIdType.MESH)
+
+        @pl.when(root)
+        def _():
+            pl.semaphore_wait(here, n_chan - 1)
+
+    def release_all():
+        @pl.when(root)
+        def _():
+            pl.semaphore_wait(barrier, n_chan * (n_dp - 1))
+
+            @pl.loop(1, n_dp)
+            def _(d):
+                for j in range(n_chan):
+                    pl.semaphore_signal(go, inc=1, device_id={"dp": d, "chan": j}, device_id_type=pl.DeviceIdType.MESH)
+
+            for j in range(1, n_chan):
+                pl.semaphore_signal(go, inc=1, device_id={"chan": j}, device_id_type=pl.DeviceIdType.MESH)
+
+    def enter_all():
+        @pl.when(jnp.logical_not(root))
+        def _():
+            pl.semaphore_wait(go, 1)
 
     def remote(src, dst, send, recv, where):
         return pltpu.make_async_remote_copy(
@@ -73,7 +131,7 @@
     for c in local:
         c.start()
 
-    pl.semaphore_wait(barrier, n_chan - 1 + n_dp - 1)
+    enter_group()
 
     xw = cells // X_PARTS
     gw = cells // G_PARTS
@@ -126,8 +184,8 @@
     def p_far_copy():
         return remote(p_half, p_in.at[parity], ps.at[1], pr.at[1], {"chan": far})
 
-    def p_diag_copy():
-        return remote(p_half, p_in.at[parity], ps.at[2], pr.at[2], {"chan": diag})
+    def p_pass_copy():
+        return remote(p_in.at[parity], p_in.at[parity], ps.at[2], pr.at[2], {"chan": core})
 
     p_core_copy().start()
 
@@ -144,7 +202,6 @@
     both = p_own[...] + p_core[...]
     p_half[...] = jnp.where(parity == 0, both[:, :quarter], both[:, quarter:])
     p_far_copy().start()
-    p_diag_copy().start()
     x_copy("y", 1).start()
     for k in range(G_PARTS):
         g_copy("c", k).start()
@@ -214,13 +271,21 @@
                     v = h
                 stack[3 * a + b, at, :] = v.astype(BF16)
 
+    p_far_copy().wait_recv()
+    p_pass_copy().start()
+    release_all()
+    x_copy("y", 3).start()
     k_all[me] = k_send[me]
 
     for a in range(3):
         v_buf[a, :, :LANES] = jnp.zeros((ch, LANES), F32)
         v_buf[a, :, LANES + cells:] = jnp.zeros((ch, LANES), F32)
 
-    s_buf[tiles // pieces:] = jnp.zeros((n_dp - tiles // pieces, pieces, SUB, LANES), F32)
+    def place(at):
+        piece = at % pieces
+        return at // pieces, piece // per, piece % per * rank
+
+    s_buf[...] = jnp.zeros(s_buf.shape, F32)
     for t in range(TAPS):
         local[3 + t].wait()
     for t in range(TAPS):
@@ -231,10 +296,10 @@
                 jnp.sum(jnp.sum((value * wide_q[r]).reshape(ch // SUB, SUB, LANES), axis=0), axis=0, keepdims=True)
                 for r in range(rank)
             ]
-            s_buf[at // pieces, at % pieces] = jnp.concatenate(sums + [jnp.zeros((SUB - rank, LANES), F32)], axis=0)
-
-    p_far_copy().wait_recv()
-    p_diag_copy().wait_recv()
+            o, c, r0 = place(at)
+            s_buf[o, c, r0:r0 + rank, :] = jnp.concatenate(sums, axis=0)
+
+    p_pass_copy().wait_recv()
     both = p_own[...] + p_core[...]
     both = jnp.concatenate([both[:, :quarter] + p_in[0], both[:, quarter:] + p_in[1]], axis=1)
     p = jnp.concatenate([both[:rank], both[rank:]], axis=1)
@@ -280,9 +345,10 @@
     for t in range(TAPS):
         for l in range(tap_tiles):
             at = t * tap_tiles + l
-            s_buf[at // pieces, at % pieces] += p_wide[t, :, l * LANES:(l + 1) * LANES]
-
-    x_copy("y", 3).start()
+            o, c, r0 = place(at)
+            s_buf[o, c, r0:r0 + rank, :] += p_wide[t, :rank, l * LANES:(l + 1) * LANES]
+
+    x_copy("y", 4).start()
 
     def forward_x(k):
         x_copy("y", k).wait_recv()
@@ -315,13 +381,15 @@
         peer = dp_peer(i)
         return remote(s_buf.at[peer], s_in.at[dp], ss.at[i - 1], sr.at[i - 1], {"dp": peer})
 
+    enter_all()
+
     @pl.loop(1, n_dp)
     def _(i):
         s_copy(i).start()
 
     forward_x(0)
     run_n(0, N_FIRST)
-    x_copy("y", 4).start()
+    x_copy("y", 5).start()
     k_across().wait_recv()
     for i in range(1, lines):
         k_line(i).start()
@@ -331,27 +399,17 @@
         g_copy("y", k).wait_recv()
         g_copy("f", k).start()
 
-    def in_grad_part(k):
+    def in_grad_arrived(k):
         g_copy("c", k).wait_recv()
         g_copy("f", k).wait_recv()
-        s = part(k, gw)
-        col = lax.broadcasted_iota(jnp.int32, (1, gw), 1) % side
-        for a in range(3):
-            y = lax.dot_general(
-                kt[3 * a * ch:(3 * a + 3) * ch, :], g_all[:, :, s].reshape(channels, gw),
-                (((1,), (0,)), ((), ())), preferred_element_type=F32,
-            )
-            left = pltpu.roll(jnp.where(col != 0, y[:ch], 0.0), gw - 1, 1)
-            right = pltpu.roll(jnp.where(col != side - 1, y[2 * ch:], 0.0), 1, 1)
-            v_buf[a, :, pl.ds(pl.multiple_of(LANES + k * gw, LANES), gw)] = left + y[ch:2 * ch] + right
+
+    def in_grad_part(k):
+        in_grad_arrived(k)
+        g_cols = g_all[:, :, part(k, gw)].reshape(channels, gw)
+        tap_rows(side, kt, g_cols, v_buf, pl.ds(pl.multiple_of(LANES + k * gw, LANES), gw))
 
     def finish_part(k):
-        base = k * gw
-        wide = gw + LANES
-        up = pltpu.roll(v_buf[0, :, pl.ds(pl.multiple_of(base + LANES, LANES), wide)], wide - side, 1)[:, :gw]
-        down = pltpu.roll(v_buf[2, :, pl.ds(pl.multiple_of(base, LANES), wide)], wide - (LANES - side), 1)[:, :gw]
-        mid = v_buf[1, :, pl.ds(pl.multiple_of(base + LANES, LANES), gw)]
-        in_grad_ref[:, part(k, gw)] = (up + mid + down).astype(BF16)
+        in_grad_ref[:, part(k, gw)] = finish_cells(side, v_buf, k * gw, gw)
 
     @pl.loop(1, n_dp)
     def _(i):
@@ -366,7 +424,7 @@
     for i in range(1, n_chan):
         c_copy(i).start()
     share_in[me] = share[...]
-    for k in range(5, X_PARTS):
+    for k in range(6, X_PARTS):
         x_copy("y", k).start()
     for k in range(G_PARTS):
         g_copy("y", k).start()
@@ -391,10 +449,10 @@
     def _(i):
         a_copy(i).wait_recv()
 
-    cols = [s_full[:, :, r, :] for r in range(rank)]
+    cols = [[s_full[:, :, u * rank + r, :] for u in range(per)] for r in range(rank)]
 
     def inner(u, v):
-        return jnp.sum(u * v).reshape(1, 1, 1)
+        return sum(jnp.sum(x * y).reshape(1, 1, 1) for x, y in zip(u, v))
 
     gram = {}
     for i in range(rank):
@@ -416,10 +474,11 @@
     for r in range(rank):
         v = cols[r]
         for m in range(r):
-            v = v - low[r, m] * base[m]
-        v = v / low[r, r]
+            v = [x - low[r, m] * y for x, y in zip(v, base[m])]
+        v = [x / low[r, r] for x in v]
         base.append(v)
-        b_ref[:, :, r, :] = v
+        for u in range(per):
+            b_ref[:, :, u * rank + r, :] = v[u]
 
     for i in range(1, lines):
         k_line(i).wait_recv()
@@ -437,8 +496,9 @@
                 lanes = slice(l * LANES, (l + 1) * LANES)
                 value = n_ref[t, rows_h, lanes] * (1.0 / side) + e_vm[t, rows_h, lanes]
                 n_ref[t, rows_h, lanes] = value
+                o, c, r0 = place(at)
                 for r in range(rank):
-                    acc[r] = acc[r] + value * b_ref[at // pieces, at % pieces, r:r + 1, :]
+                    acc[r] = acc[r] + value * b_ref[o, c, r0 + r:r0 + r + 1, :]
         block = jnp.zeros((half, LANES), F32)
         for r in range(rank):
             block = jnp.where(lane == r, jnp.sum(acc[r], axis=1, keepdims=True), block)
@@ -474,25 +534,23 @@
             at = t * tap_tiles + l
             lanes = slice(l * LANES, (l + 1) * LANES)
             value = n_ref[t, :, lanes]
+            o, c, r0 = place(at)
             for r in range(rank):
-                value = value - wide_q[r] * b_ref[at // pieces, at % pieces, r:r + 1, :]
+                value = value - wide_q[r] * b_ref[o, c, r0 + r:r0 + r + 1, :]
             n_ref[t, :, lanes] = value
 
     forward_g(0)
 
-    @pl.loop(0, G_PARTS)
+    @pl.loop(0, G_PARTS - 1)
     def _(k):
-        @pl.when(k + 1 < G_PARTS)
-        def _():
-            forward_g(k + 1)
-
+        forward_g(k + 1)
         in_grad_part(k)
 
         @pl.when(k > 0)
         def _():
             finish_part(k - 1)
 
-    finish_part(G_PARTS - 1)
+    in_grad_arrived(G_PARTS - 1)
 
     @pl.loop(0, X_PARTS)
     def _(k):
@@ -512,7 +570,7 @@
     k_across().wait_send()
     p_core_copy().wait_send()
     p_far_copy().wait_send()
-    p_diag_copy().wait_send()
+    p_pass_copy().wait_send()
     for i in range(1, lines):
         k_line(i).wait_send()
     for i in range(lines):
@@ -525,18 +583,29 @@
         f_copy(i).wait_send()
 
 
-def write_body(in_grad_vm, qf_vm, n_vm, in_grad_hbm, qf_hbm, err_hbm, sem):
+def tail_body(side, in_grad_vm, qf_vm, n_vm, g_vm, kt_vm, v_vm, in_grad_hbm, qf_hbm, err_hbm, v_tail, out, sem):
+    n_chan, ch, cells = g_vm.shape
     channels = n_vm.shape[2]
+    gw = cells // G_PARTS
+    done = cells - 2 * gw
     copies = [
         pltpu.make_async_copy(n_vm.at[t], err_hbm.at[0, :, pl.ds(t * channels, channels)], sem.at[t])
         for t in range(TAPS)
     ]
-    copies.append(pltpu.make_async_copy(in_grad_vm, in_grad_hbm, sem.at[TAPS]))
-    copies.append(pltpu.make_async_copy(qf_vm, qf_hbm, sem.at[TAPS + 1]))
+    copies.append(pltpu.make_async_copy(qf_vm, qf_hbm, sem.at[TAPS]))
+    copies.append(pltpu.make_async_copy(in_grad_vm, in_grad_hbm.at[:, :done], sem.at[TAPS + 1]))
     for c in copies:
         c.start()
+    v_tail[:, :, :LANES + gw] = v_vm[:, :, done:done + LANES + gw]
+    v_tail[:, :, LANES + 2 * gw:] = jnp.zeros((3, ch, LANES), F32)
+    tap_rows(side, kt_vm, g_vm[:, :, done + gw:].reshape(channels, gw), v_tail, slice(LANES + gw, LANES + 2 * gw))
+    for k in range(2):
+        out[:, k * gw:(k + 1) * gw] = finish_cells(side, v_tail, k * gw, gw)
+    last = pltpu.make_async_copy(out, in_grad_hbm.at[:, done:], sem.at[TAPS + 2])
+    last.start()
     for c in copies:
         c.wait()
+    last.wait()
 
 
 def per_device(activations, out_grad, kernel, error_in, q_prev):
@@ -546,8 +615,10 @@
     channels = kernel.shape[1] // TAPS
     rank = q_prev.shape[1]
     side = round(cells ** 0.5)
+    gw = cells // G_PARTS
     tiles = channels * TAPS // LANES
     pieces = -(-tiles // n_dp)
+    packs = -(-pieces // (SUB // rank))
     kw = -(-TAPS * ch // LANES) * LANES
     fw = -(-ch // LANES) * LANES
     qt = q_prev.T
@@ -558,28 +629,28 @@
     held = pl.pallas_call(
         functools.partial(kernel_body, (n_dp, n_chan, side, rank, pieces)),
         out_shape=(
-            pltpu.VMEM((ch, cells), BF16),
+            pltpu.VMEM((ch, cells - 2 * gw), BF16),
             pltpu.VMEM((rank, ch), F32),
             pltpu.VMEM((TAPS, ch, channels), F32),
+            pltpu.VMEM((n_chan, ch, cells), BF16),
+            pltpu.VMEM((kw, channels), BF16),
+            pltpu.VMEM((3, ch, cells + 2 * LANES), F32),
         ),
         in_specs=[anyspace, anyspace, anyspace, anyspace, vmem],
-        out_specs=(vmem, vmem, vmem),
+        out_specs=(vmem,) * 6,
         scratch_shapes=[
-            pltpu.VMEM((n_chan, ch, cells), BF16),
             pltpu.VMEM((n_chan, ch, cells), BF16),
             pltpu.VMEM((TAPS, ch, cells), BF16),
             pltpu.VMEM((TAPS, ch, channels), F32),
             pltpu.VMEM(kernel.shape, BF16),
             pltpu.VMEM((n_chan, ch, kw), BF16),
             pltpu.VMEM((n_chan, ch, kw), BF16),
-            pltpu.VMEM((kw, channels), BF16),
-            pltpu.VMEM((3, ch, cells + 2 * LANES), F32),
-            pltpu.VMEM((n_dp, pieces, SUB, LANES), F32),
-            pltpu.VMEM((n_dp, pieces, SUB, LANES), F32),
-            pltpu.VMEM((pieces, SUB, LANES), F32),
-            pltpu.VMEM((n_chan, pieces, SUB, LANES), F32),
-            pltpu.VMEM((n_dp, pieces, SUB, LANES), F32),
-            pltpu.VMEM((n_dp, pieces, SUB, LANES), F32),
+            pltpu.VMEM((n_dp, packs, SUB, LANES), F32),
+            pltpu.VMEM((n_dp, packs, SUB, LANES), F32),
+            pltpu.VMEM((packs, SUB, LANES), F32),
+            pltpu.VMEM((n_chan, packs, SUB, LANES), F32),
+            pltpu.VMEM((n_dp, packs, SUB, LANES), F32),
+            pltpu.VMEM((n_dp, packs, SUB, LANES), F32),
             pltpu.VMEM((n_dp, SUB, fw), F32),
             pltpu.VMEM((rank, ch, LANES), F32),
             pltpu.VMEM((2 * rank, cells // 2), F32),
@@ -597,22 +668,27 @@
         + [dma((n_dp - 1,))] * 2
         + [dma((n_chan - 1,))] * 2
         + [dma((n_dp - 1,))] * 4
-        + [dma((GROUP - 1,))] * 2,
+        + [dma((GROUP - 1,))] * 2
+        + [pltpu.SemaphoreType.REGULAR] * 2,
         compiler_params=pltpu.CompilerParams(
-            collective_id=0, has_side_effects=True, vmem_limit_bytes=56000000
+            collective_id=0, has_side_effects=True, vmem_limit_bytes=42000000
         ),
     )(activations, out_grad, kernel, error_in, qt)
     in_grad, qf_t, new_error = pl.pallas_call(
-        write_body,
+        functools.partial(tail_body, side),
         out_shape=(
             jax.ShapeDtypeStruct((ch, cells), BF16),
             jax.ShapeDtypeStruct((rank, ch), F32),
             jax.ShapeDtypeStruct(error_in.shape, F32),
         ),
-        in_specs=[vmem, vmem, vmem],
+        in_specs=[vmem] * 6,
         out_specs=(anyspace, anyspace, anyspace),
-        scratch_shapes=[dma((TAPS + 2,))],
-        compiler_params=pltpu.CompilerParams(vmem_limit_bytes=1000000),
+        scratch_shapes=[
+            pltpu.VMEM((3, ch, 2 * gw + 2 * LANES), F32),
+            pltpu.VMEM((ch, 2 * gw), BF16),
+            dma((TAPS + 3,)),
+        ],
+        compiler_params=pltpu.CompilerParams(vmem_limit_bytes=12000000),
     )(*held)
     return in_grad, qf_t.T, new_error
 

time: 80.6 us -> 76.4 us (0.948)
  Pallas kernels: 79.3 us -> 75.1 us
    pallas_call x1, Pallas kernels: 76.9 us -> 71.3 us  [per_device(): pl.pallas_call(functools.partial(kernel_body, (n_dp, n_chan, side, rank,...]
    pallas_call x1, Pallas kernels: 2.37 us -> 3.77 us  [per_device(): pl.pallas_call(functools.partial(tail_body, side), out_shape=(jax.ShapeDt...]
where the time goes in v3:
time: 76.4 us; the launch traced here: 75.9 us
  Pallas kernels  75.1 us (98%)
  between operations  0.8 us (1%)
    pallas_call x1, Pallas kernels, per_device(): pl.pallas_call(functools.partial(kernel_body, (n_dp, n_chan, side, rank,...  71.3 us
    pallas_call x1, Pallas kernels, per_device(): pl.pallas_call(functools.partial(tail_body, side), out_shape=(jax.ShapeDt...  3.77 us

profile of v3, /device:TPU:0, one launch (start us, length us, event | category | flops | bytes accessed | tf_op | source)
XLA Modules:
  0.0 75.9 jit_solution(7711576469974295450)
XLA Ops:
  0.6 71.3 %shard_map.76 = (bf16[160,3072]{1,0:T(8,128)(2,1)S(1)}, f32[4,160]{1,0:T(4,128)S(1)}, f32[9,160,640]{2,1,0:T(8,128)S(1)}, bf16[4,160,4096]{2,1,0:T(8,128)(2,1)S(...) custom-call(bf16[160,4096]{1,0:T(8,128)(2,1)} %x_hbm.1, bf16[160,4096]{1,0:T(8,128)(2,1)} %g_hbm.1, ...), custom_call_target="tpu_custom_call" | custom-call | tf_op jit(solution)/shard_map/pallas_call | solution.py:629
  72.0 3.8 %shard_map.77 = (bf16[160,4096]{1,0:T(8,128)(2,1)}, f32[4,160]{1,0:T(4,128)}, f32[1,160,5760]{2,1,0:T(8,128)}) custom-call(bf16[160,3072]{1,0:T(8,128)(2,1)S(1)} %get-tuple-element.12.in_grad_vm, f32[4,160]{1,0:T(4,128)S(1)} %get-tuple-element.13.qf_vm, f32[9,160,640]{2,1,0:T(8,128)S(1)} %get-tuple-element.14.n_vm, ...), custom_call_target="tpu_custom_call" | custom-call | tf_op jit(solution)/shard_map/pallas_call | solution.py:677

commit v4 on v3

--- a/solution.py
+++ b/solution.py
@@ -16,6 +16,7 @@
 N_SECOND = 2
 N_THIRD = 3
 GROUP = 8
+G_SPLIT = 3
 HI = lax.Precision.HIGHEST
 F32 = jnp.float32
 BF16 = jnp.bfloat16
@@ -147,13 +148,17 @@
             return remote(x_hbm.at[:, s], x_all.at[me, :, s], xs_c.at[k], xr_c.at[k], {"chan": core})
         return remote(x_all.at[far, :, s], x_all.at[far, :, s], xs_f.at[k], xr_f.at[k], {"chan": core})
 
-    def g_copy(kind, k):
-        s = part(k, gw)
+    def g_copy(kind, k, w=gw, at=None):
+        s = part(k, w)
+        at = k if at is None else at
         if kind == "y":
-            return remote(g_hbm.at[:, s], g_all.at[me, :, s], gs_y.at[k], gr_y.at[k], {"chan": far})
+            return remote(g_hbm.at[:, s], g_all.at[me, :, s], gs_y.at[at], gr_y.at[at], {"chan": far})
         if kind == "c":
-            return remote(g_hbm.at[:, s], g_all.at[me, :, s], gs_c.at[k], gr_c.at[k], {"chan": core})
-        return remote(g_all.at[far, :, s], g_all.at[far, :, s], gs_f.at[k], gr_f.at[k], {"chan": core})
+            return remote(g_hbm.at[:, s], g_all.at[me, :, s], gs_c.at[at], gr_c.at[at], {"chan": core})
+        return remote(g_all.at[far, :, s], g_all.at[far, :, s], gs_f.at[at], gr_f.at[at], {"chan": core})
+
+    def g_tail(kind, j):
+        return g_copy(kind, 2 * (G_PARTS - 1) + j, gw // 2, G_PARTS - 1 + j)
 
     x_copy("y", 0).start()
     for k in range(X_PARTS):
@@ -411,6 +416,24 @@
     def finish_part(k):
         in_grad_ref[:, part(k, gw)] = finish_cells(side, v_buf, k * gw, gw)
 
+    def run_parts(begin, end):
+        @pl.loop(begin, end)
+        def _(k):
+            @pl.when(k + 1 < G_PARTS - 1)
+            def _():
+                forward_g(k + 1)
+
+            @pl.when(k + 1 == G_PARTS - 1)
+            def _():
+                g_tail("y", 0).wait_recv()
+                g_tail("f", 0).start()
+
+            in_grad_part(k)
+
+            @pl.when(k > 0)
+            def _():
+                finish_part(k - 1)
+
     @pl.loop(1, n_dp)
     def _(i):
         s_copy(i).wait_recv()
@@ -426,8 +449,10 @@
     share_in[me] = share[...]
     for k in range(6, X_PARTS):
         x_copy("y", k).start()
-    for k in range(G_PARTS):
+    for k in range(G_PARTS - 1):
         g_copy("y", k).start()
+    for j in range(2):
+        g_tail("y", j).start()
     run_n(N_FIRST, N_SECOND)
     for i in range(1, n_chan):
         c_copy(i).wait_recv()
@@ -522,6 +547,9 @@
         block = k_all[:, :, i * LANES:(i + 1) * LANES].reshape(channels, LANES)
         kt[i * LANES:(i + 1) * LANES, :] = jnp.transpose(block)
 
+    forward_g(0)
+    run_parts(0, G_SPLIT)
+
     @pl.loop(1, n_dp)
     def _(i):
         f_copy(i).wait_recv()
@@ -539,18 +567,16 @@
                 value = value - wide_q[r] * b_ref[o, c, r0 + r:r0 + r + 1, :]
             n_ref[t, :, lanes] = value
 
-    forward_g(0)
-
-    @pl.loop(0, G_PARTS - 1)
-    def _(k):
-        forward_g(k + 1)
-        in_grad_part(k)
-
-        @pl.when(k > 0)
-        def _():
-            finish_part(k - 1)
-
-    in_grad_arrived(G_PARTS - 1)
+    run_parts(G_SPLIT, G_PARTS - 1)
+    g_tail("y", 1).wait_recv()
+    g_tail("f", 1).start()
+    g_copy("c", G_PARTS - 1).wait_recv()
+    g_tail("f", 0).wait_recv()
+    a0 = (G_PARTS - 1) * gw
+    tw = gw // 2
+    tap_rows(side, kt, g_all[:, :, a0:a0 + tw].reshape(channels, tw), v_buf, slice(LANES + a0, LANES + a0 + tw))
+    finish_part(G_PARTS - 2)
+    g_tail("f", 1).wait_recv()
 
     @pl.loop(0, X_PARTS)
     def _(k):
@@ -560,9 +586,16 @@
 
     @pl.loop(0, G_PARTS)
     def _(k):
+        g_copy("c", k).wait_send()
+
+    @pl.loop(0, G_PARTS - 1)
+    def _(k):
         g_copy("y", k).wait_send()
-        g_copy("c", k).wait_send()
         g_copy("f", k).wait_send()
+
+    for j in range(2):
+        g_tail("y", j).wait_send()
+        g_tail("f", j).wait_send()
 
     for i in range(1, n_chan):
         c_copy(i).wait_send()
@@ -586,7 +619,7 @@
 def tail_body(side, in_grad_vm, qf_vm, n_vm, g_vm, kt_vm, v_vm, in_grad_hbm, qf_hbm, err_hbm, v_tail, out, sem):
     n_chan, ch, cells = g_vm.shape
     channels = n_vm.shape[2]
-    gw = cells // G_PARTS
+    gw = cells // G_PARTS // 2
     done = cells - 2 * gw
     copies = [
         pltpu.make_async_copy(n_vm.at[t], err_hbm.at[0, :, pl.ds(t * channels, channels)], sem.at[t])
@@ -629,7 +662,7 @@
     held = pl.pallas_call(
         functools.partial(kernel_body, (n_dp, n_chan, side, rank, pieces)),
         out_shape=(
-            pltpu.VMEM((ch, cells - 2 * gw), BF16),
+            pltpu.VMEM((ch, cells - gw), BF16),
             pltpu.VMEM((rank, ch), F32),
             pltpu.VMEM((TAPS, ch, channels), F32),
             pltpu.VMEM((n_chan, ch, cells), BF16),
@@ -663,7 +696,7 @@
             dma((3 + TAPS,)),
         ]
         + [dma((X_PARTS,))] * 6
-        + [dma((G_PARTS,))] * 6
+        + [dma((G_PARTS + 1,))] * 6
         + [dma((n_chan - 1,))] * 4
         + [dma((n_dp - 1,))] * 2
         + [dma((n_chan - 1,))] * 2
@@ -684,8 +717,8 @@
         in_specs=[vmem] * 6,
         out_specs=(anyspace, anyspace, anyspace),
         scratch_shapes=[
-            pltpu.VMEM((3, ch, 2 * gw + 2 * LANES), F32),
-            pltpu.VMEM((ch, 2 * gw), BF16),
+            pltpu.VMEM((3, ch, gw + 2 * LANES), F32),
+            pltpu.VMEM((ch, gw), BF16),
             dma((TAPS + 3,)),
         ],
         compiler_params=pltpu.CompilerParams(vmem_limit_bytes=12000000),

time: 76.4 us -> 74.7 us (0.978)
  Pallas kernels: 75.1 us -> 73.7 us
    pallas_call x1, Pallas kernels: 71.3 us -> 70.5 us  [per_device(): pl.pallas_call(functools.partial(kernel_body, (n_dp, n_chan, side, rank,...]
where the time goes in v4:
time: 74.7 us; the launch traced here: 74.5 us
  Pallas kernels  73.7 us (99%)
  between operations  0.82 us (1%)
    pallas_call x1, Pallas kernels, per_device(): pl.pallas_call(functools.partial(kernel_body, (n_dp, n_chan, side, rank,...  70.5 us
    pallas_call x1, Pallas kernels, per_device(): pl.pallas_call(functools.partial(tail_body, side), out_shape=(jax.ShapeDt...  3.19 us

profile of v4, /device:TPU:0, one launch (start us, length us, event | category | flops | bytes accessed | tf_op | source)
XLA Modules:
  0.0 74.5 jit_solution(13699618479684387752)
XLA Ops:
  0.6 70.5 %shard_map.76 = (bf16[160,3584]{1,0:T(8,128)(2,1)S(1)}, f32[4,160]{1,0:T(4,128)S(1)}, f32[9,160,640]{2,1,0:T(8,128)S(1)}, bf16[4,160,4096]{2,1,0:T(8,128)(2,1)S(...) custom-call(bf16[160,4096]{1,0:T(8,128)(2,1)} %x_hbm.1, bf16[160,4096]{1,0:T(8,128)(2,1)} %g_hbm.1, ...), custom_call_target="tpu_custom_call" | custom-call | tf_op jit(solution)/shard_map/pallas_call | solution.py:662
  71.2 3.2 %shard_map.77 = (bf16[160,4096]{1,0:T(8,128)(2,1)}, f32[4,160]{1,0:T(4,128)}, f32[1,160,5760]{2,1,0:T(8,128)}) custom-call(bf16[160,3584]{1,0:T(8,128)(2,1)S(1)} %get-tuple-element.12.in_grad_vm, f32[4,160]{1,0:T(4,128)S(1)} %get-tuple-element.13.qf_vm, f32[9,160,640]{2,1,0:T(8,128)S(1)} %get-tuple-element.14.n_vm, ...), custom_call_target="tpu_custom_call" | custom-call | tf_op jit(solution)/shard_map/pallas_call | solution.py:710

commit v5 on v4

--- a/solution.py
+++ b/solution.py
@@ -14,7 +14,7 @@
 G_PARTS = 8
 N_FIRST = 1
 N_SECOND = 2
-N_THIRD = 3
+N_THIRD = 5
 GROUP = 8
 G_SPLIT = 3
 HI = lax.Precision.HIGHEST

time: 74.7 us -> 72.6 us (0.972)
  Pallas kernels: 73.7 us -> 71.6 us
    pallas_call x1, Pallas kernels: 70.5 us -> 68.4 us  [per_device(): pl.pallas_call(functools.partial(kernel_body, (n_dp, n_chan, side, rank,...]
where the time goes in v5:
time: 72.6 us; the launch traced here: 72.4 us
  Pallas kernels  71.6 us (99%)
  between operations  0.82 us (1%)
    pallas_call x1, Pallas kernels, per_device(): pl.pallas_call(functools.partial(kernel_body, (n_dp, n_chan, side, rank,...  68.4 us
    pallas_call x1, Pallas kernels, per_device(): pl.pallas_call(functools.partial(tail_body, side), out_shape=(jax.ShapeDt...  3.19 us

profile of v5, /device:TPU:0, one launch (start us, length us, event | category | flops | bytes accessed | tf_op | source)
XLA Modules:
  0.0 72.4 jit_solution(11793228340068063840)
XLA Ops:
  0.6 68.4 %shard_map.76 = (bf16[160,3584]{1,0:T(8,128)(2,1)S(1)}, f32[4,160]{1,0:T(4,128)S(1)}, f32[9,160,640]{2,1,0:T(8,128)S(1)}, bf16[4,160,4096]{2,1,0:T(8,128)(2,1)S(...) custom-call(bf16[160,4096]{1,0:T(8,128)(2,1)} %x_hbm.1, bf16[160,4096]{1,0:T(8,128)(2,1)} %g_hbm.1, ...), custom_call_target="tpu_custom_call" | custom-call | tf_op jit(solution)/shard_map/pallas_call | solution.py:662
  69.0 3.2 %shard_map.77 = (bf16[160,4096]{1,0:T(8,128)(2,1)}, f32[4,160]{1,0:T(4,128)}, f32[1,160,5760]{2,1,0:T(8,128)}) custom-call(bf16[160,3584]{1,0:T(8,128)(2,1)S(1)} %get-tuple-element.12.in_grad_vm, f32[4,160]{1,0:T(4,128)S(1)} %get-tuple-element.13.qf_vm, f32[9,160,640]{2,1,0:T(8,128)S(1)} %get-tuple-element.14.n_vm, ...), custom_call_target="tpu_custom_call" | custom-call | tf_op jit(solution)/shard_map/pallas_call | solution.py:710
